TPU v7x, 32 devices: a whole 2x2x4 slice. The times are simulated.
32 devices in a mesh: path: 4 (over z), trade: 8 (over y, x, core).
Axes of the slice: x: 2, y: 2, z: 4, core: 2. Of those that a mesh axis runs over, the one named last changes fastest.
Arguments:
- factors: bfloat16 [32, 8, 512], P(None, None, 'path'), may hold values from -5 to 5
- loadings: bfloat16 [32, 8, 32768], P(None, None, 'trade'), may hold values from -0.5 to 0.5
- notional: float32 [32768], P('trade'), may hold values from -1 to 1
- strike: float32 [32768], P('trade'), may hold values from 0.5 to 1.5
- date_weight: float32 [32], replicated, may hold values from 0.3 to 3
- loss_spanning: float32 [128], replicated, may hold values from 0.2 to 0.9
- loss_local: float32 [1024], P('trade'), may hold values from 0.2 to 0.9
- trade_slot: int32 [32768], P('trade'), may hold values from 0 to 255
- span_list: int32 [1024], P('trade'), may hold values from 0 to 127, as said below
Outputs:
- loading_grad: float32 [32, 8, 32768], P('path', None, 'trade')
- factor_grad: float32 [32, 8, 512], P('trade', None, 'path')
Inputs may be any that keep to these rules, and one draw needn't show every extreme that they name: `trade_slot`: slot s < 128 of a trade shard holds that shard's spanning set from span_list; slot 128 + i holds the shard's i-th local set. `span_list`: the 128 entries of one trade shard are distinct spanning set ids.
All inputs are finite; a program needn't handle non-finite values.
Results may differ from a plain program's by a relative error of at most 0.0021.
Values may be sent and summed in bfloat16 or wider, within the bound.
A program may use at most 64 MiB of HBM per device.

v0:
```python
import functools
import math

import jax
import jax.numpy as jnp
from jax import lax
from jax.experimental import pallas as pl
from jax.experimental.pallas import tpu as pltpu
from jax.sharding import PartitionSpec as P

smoothing = 0.5
MESH = pl.DeviceIdType.MESH
bf16 = jnp.bfloat16
f32 = jnp.float32


def chunk_of(paths, trades):
    return math.gcd(trades, (1 << 20) // paths)


def dot(a, b):
    return jnp.dot(a, b, preferred_element_type=f32)


def kernel(
    n_path,
    n_trade,
    factors_ref,
    loadings_ref,
    notional_ref,
    strike_ref,
    date_weight_ref,
    loss_span_ref,
    loss_local_ref,
    slot_ref,
    span_ref,
    loading_grad_ref,
    factor_grad_ref,
    growth,
    table,
    table_t,
    load_own,
    load_wide,
    offset,
    fac_recv,
    fac,
    fac_t,
    total,
    part,
    pair_recv,
    chip_sum,
    cross_recv,
    local_w,
    span_half,
    span_other,
    slot_w,
    factor_acc,
    grad_send,
    grad_recv,
    load_sem,
    fac_ssem,
    fac_rsem,
    pair_ssem,
    pair_rsem,
    cross_ssem,
    cross_rsem,
    half_ssem,
    half_rsem,
    other_ssem,
    other_rsem,
    grad_ssem,
    grad_rsem,
):
    me_path = lax.axis_index("path")
    me_trade = lax.axis_index("trade")
    dates, factor_count, path_local = factors_ref.shape
    dates_own = dates // n_path
    dates_out = dates // n_trade
    groups = dates_own // dates_out
    trades = loadings_ref.shape[2]
    spans = loss_span_ref.shape[1]
    span_slots = span_ref.shape[1]
    locals_ = loss_local_ref.shape[1]
    slots = span_slots + locals_
    path_total = n_path * path_local
    chunk = chunk_of(path_total, trades)
    steps = trades // chunk
    first_date = me_path * dates_own
    rows = path_total // n_trade
    chips = n_trade // 2
    me_chip = me_trade // 2
    me_core = lax.rem(me_trade, 2)
    sibling = me_trade + 1 - 2 * me_core

    def path_at(step):
        return lax.rem(me_path + step + n_path, n_path)

    def trade_at(step):
        return lax.rem(me_trade + step + n_trade, n_trade)

    def chip_at(step):
        return lax.rem(me_chip + step + chips, chips)

    def columns(c):
        return pl.ds(pl.multiple_of(c * chunk, chunk), chunk)

    load = pltpu.make_async_copy(
        loadings_ref.at[pl.ds(first_date, dates_own)], load_own, load_sem
    )
    load.start()

    barrier = pltpu.get_barrier_semaphore()
    for a in range(n_path):
        for b in range(n_trade):
            if a or b:
                pl.semaphore_signal(
                    barrier,
                    inc=1,
                    device_id={"path": path_at(a), "trade": trade_at(b)},
                    device_id_type=MESH,
                )
    set_match = (
        lax.broadcasted_iota(jnp.int32, (spans, span_slots), 0) == span_ref[...]
    ).astype(f32).astype(bf16)

    @pl.loop(0, steps)
    def _(c):
        cols = columns(c)
        hot = (
            lax.broadcasted_iota(jnp.int32, (slots, chunk), 0) == slot_ref[:, cols]
        ).astype(f32)
        span_hot = dot(set_match, hot[:span_slots].astype(bf16))
        both = jnp.concatenate([span_hot, hot[span_slots:]], axis=0)
        table_t[:, cols] = both.astype(bf16)
        table[cols, :] = both.T.astype(bf16)

    pl.semaphore_wait(barrier, n_path * n_trade - 1)

    def fac_copy(o):
        there = path_at(o)
        return pltpu.make_async_remote_copy(
            src_ref=factors_ref.at[pl.ds(there * dates_own, dates_own)],
            dst_ref=fac_recv.at[o - 1],
            send_sem=fac_ssem,
            recv_sem=fac_rsem,
            device_id={"path": there},
            device_id_type=MESH,
        )

    for o in range(1, n_path):
        fac_copy(o).start()

    offset[...] = notional_ref[...] * strike_ref[...]
    load.wait()

    for d in range(dates_own):
        row = load_own[d]
        load_wide[d] = jnp.concatenate([row, row, row, row], axis=0)

    if n_path > 1:
        pltpu.make_async_copy(fac_recv, fac_recv, fac_rsem).wait()

    for d in range(dates_own):
        blocks = [factors_ref[first_date + d]]
        blocks += [fac_recv[o - 1, d] for o in range(1, n_path)]
        whole = jnp.concatenate(blocks, axis=1)
        fac[d] = whole
        scaled = whole.astype(f32) * f32(math.log2(math.e))
        high = scaled.astype(bf16).astype(f32)
        middle = (scaled - high).astype(bf16).astype(f32)
        low = scaled - high - middle
        split = jnp.concatenate([high, middle, low, jnp.zeros_like(low)], axis=0)
        fac_t[d] = split.T.astype(bf16)

    def wait_all(buffer, sem):
        pltpu.make_async_copy(buffer, buffer, sem).wait()

    def send_pair(d):
        pltpu.make_async_remote_copy(
            src_ref=part.at[d, 1 - me_core],
            dst_ref=pair_recv.at[d],
            send_sem=pair_ssem.at[d],
            recv_sem=pair_rsem.at[d],
            device_id={"trade": sibling},
            device_id_type=MESH,
        ).start()

    def send_cross(d):
        wait_all(pair_recv.at[d], pair_rsem.at[d])
        chip_sum[d] = part[d, me_core] + pair_recv[d]
        for o in range(1, chips):
            there = chip_at(o)
            pltpu.make_async_remote_copy(
                src_ref=chip_sum.at[d, there],
                dst_ref=cross_recv.at[d, o - 1],
                send_sem=cross_ssem.at[d],
                recv_sem=cross_rsem.at[d],
                device_id={"trade": there * 2 + me_core},
                device_id_type=MESH,
            ).start()

    def send_half(d):
        wait_all(cross_recv.at[d], cross_rsem.at[d])
        sums = chip_sum[d, me_chip]
        for o in range(1, chips):
            sums = sums + cross_recv[d, o - 1]
        weight = date_weight_ref[first_date + d]
        span_half[d, 0] = (
            weight * loss_span_ref[...] * jax.nn.sigmoid(sums / smoothing)
        ).astype(bf16)
        for o in range(1, chips):
            pltpu.make_async_remote_copy(
                src_ref=span_half.at[d, 0],
                dst_ref=span_half.at[d, o],
                send_sem=half_ssem.at[d],
                recv_sem=half_rsem.at[d],
                device_id={"trade": chip_at(o) * 2 + me_core},
                device_id_type=MESH,
            ).start()

    def send_other(d):
        wait_all(span_half.at[d, pl.ds(1, chips - 1)], half_rsem.at[d])
        pltpu.make_async_remote_copy(
            src_ref=span_half.at[d],
            dst_ref=span_other.at[d],
            send_sem=other_ssem.at[d],
            recv_sem=other_rsem.at[d],
            device_id={"trade": sibling},
            device_id_type=MESH,
        ).start()

    lag = max(1, (dates_own - 1) // 3)
    stages = ((lag, send_cross), (2 * lag, send_half), (3 * lag, send_other))

    @pl.loop(0, dates_own)
    def _(d):
        total[...] = jnp.zeros_like(total)

        @pl.loop(0, steps, unroll=True)
        def _(c):
            cols = columns(c)
            exponent = dot(fac_t[d], load_wide[d, :, cols])
            grown = jnp.exp2(exponent) * notional_ref[:, cols]
            growth[d * steps + c] = grown.astype(bf16)
            values = (grown - offset[:, cols]).astype(bf16)
            total[...] += dot(values, table[cols, :])

        for r in range(n_trade):
            part[d, r % 2, r // 2] = total[r * rows : (r + 1) * rows, :spans]
        send_pair(d)
        weight = date_weight_ref[first_date + d]
        local_w[d] = (
            weight * loss_local_ref[...] * jax.nn.sigmoid(total[:, spans:] / smoothing)
        ).astype(bf16)

        for late, stage in stages:

            @pl.when(d >= late)
            def _(late=late, stage=stage):
                stage(d - late)

    def grad_copy(g, o):
        return pltpu.make_async_remote_copy(
            src_ref=grad_send.at[g, o],
            dst_ref=grad_recv.at[me_trade],
            send_sem=grad_ssem.at[g, o],
            recv_sem=grad_rsem.at[me_trade],
            device_id={"path": path_at(-o), "trade": me_path * groups + g},
            device_id_type=MESH,
        )

    @pl.loop(0, dates_own)
    def _(d):
        wait_all(span_other.at[d], other_rsem.at[d])
        for o in range(chips):
            for core, source in ((me_core, span_half), (1 - me_core, span_other)):
                start = pl.multiple_of((chip_at(-o) * 2 + core) * rows, rows)
                slot_w[pl.ds(start, rows), :spans] = source[d, o]
        slot_w[:, spans:] = local_w[d]
        factor_acc[...] = jnp.zeros_like(factor_acc)

        @pl.loop(0, steps, unroll=True)
        def _(c):
            cols = columns(c)
            weight = dot(slot_w[...], table_t[:, cols]).astype(bf16)
            sensitivity = weight * growth[d * steps + c]
            loading_grad_ref[d, :, cols] = dot(fac[d], sensitivity) / path_total
            factor_acc[...] += lax.dot_general(
                load_own[d, :, cols],
                sensitivity,
                (((1,), (1,)), ((), ())),
                preferred_element_type=f32,
            )

        g = d // dates_out
        for o in range(n_path):
            grad_send[g, o, lax.rem(d, dates_out)] = factor_acc[
                :, o * path_local : (o + 1) * path_local
            ]

        for late, stage in stages:

            @pl.when(d < late)
            def _(late=late, stage=stage):
                stage(d + dates_own - late)

        @pl.when(lax.rem(d, dates_out) == dates_out - 1)
        def _():
            here = me_path * groups + g == me_trade

            @pl.when(here)
            def _():
                pltpu.make_async_copy(
                    grad_send.at[g, 0], grad_recv.at[me_trade], grad_rsem.at[me_trade]
                ).start()

            @pl.when(jnp.logical_not(here))
            def _():
                grad_copy(g, 0).start()

            for o in range(1, n_path):
                grad_copy(g, o).start()

    if n_path > 1:
        wait_all(fac_recv, fac_ssem)
    for d in range(dates_own):
        wait_all(pair_recv.at[d], pair_ssem.at[d])
        wait_all(cross_recv.at[d], cross_ssem.at[d])
        wait_all(span_half.at[d, pl.ds(1, chips - 1)], half_ssem.at[d])
        wait_all(span_other.at[d], other_ssem.at[d])
    for g in range(groups):

        @pl.when(me_path * groups + g != me_trade)
        def _():
            grad_copy(g, 0).wait_send()

        for o in range(1, n_path):
            grad_copy(g, o).wait_send()

    for b in range(n_trade):
        wait_all(grad_recv.at[b], grad_rsem.at[b])
    sums = grad_recv[0]
    for b in range(1, n_trade):
        sums = sums + grad_recv[b]
    factor_grad_ref[...] = sums


def on_device(
    n_path,
    n_trade,
    factors,
    loadings,
    notional,
    strike,
    date_weight,
    loss_spanning,
    loss_local,
    trade_slot,
    span_list,
):
    dates, factor_count, path_local = factors.shape
    trades = loadings.shape[2]
    spans = loss_spanning.shape[0]
    locals_ = loss_local.shape[0]
    width = spans + locals_
    paths = n_path * path_local
    rows = paths // n_trade
    chips = n_trade // 2
    dates_own = dates // n_path
    dates_out = dates // n_trade
    groups = dates_own // dates_out
    chunk = chunk_of(paths, trades)
    vmem = pl.BlockSpec(memory_space=pltpu.VMEM)
    dma = pltpu.SemaphoreType.DMA
    return pl.pallas_call(
        functools.partial(kernel, n_path, n_trade),
        out_shape=(
            pltpu.VMEM((dates_own, factor_count, trades), f32),
            pltpu.VMEM((dates_out, factor_count, path_local), f32),
        ),
        in_specs=[
            vmem,
            pl.BlockSpec(memory_space=pl.ANY),
            vmem,
            vmem,
            pl.BlockSpec(memory_space=pltpu.SMEM),
            vmem,
            vmem,
            vmem,
            vmem,
        ],
        out_specs=(vmem, vmem),
        scratch_shapes=[
            pltpu.VMEM((dates_own * (trades // chunk), paths, chunk), bf16),
            pltpu.VMEM((trades, width), bf16),
            pltpu.VMEM((width, trades), bf16),
            pltpu.VMEM((dates_own, factor_count, trades), bf16),
            pltpu.VMEM((dates_own, 4 * factor_count, trades), bf16),
            pltpu.VMEM((1, trades), f32),
            pltpu.VMEM((max(n_path - 1, 1), dates_own, factor_count, path_local), bf16),
            pltpu.VMEM((dates_own, factor_count, paths), bf16),
            pltpu.VMEM((dates_own, paths, 4 * factor_count), bf16),
            pltpu.VMEM((paths, width), f32),
            pltpu.VMEM((dates_own, 2, chips, rows, spans), f32),
            pltpu.VMEM((dates_own, chips, rows, spans), f32),
            pltpu.VMEM((dates_own, chips, rows, spans), f32),
            pltpu.VMEM((dates_own, chips - 1, rows, spans), f32),
            pltpu.VMEM((dates_own, paths, locals_), bf16),
            pltpu.VMEM((dates_own, chips, rows, spans), bf16),
            pltpu.VMEM((dates_own, chips, rows, spans), bf16),
            pltpu.VMEM((paths, width), bf16),
            pltpu.VMEM((factor_count, paths), f32),
            pltpu.VMEM((groups, n_path, dates_out, factor_count, path_local), f32),
            pltpu.VMEM((n_trade, dates_out, factor_count, path_local), f32),
            dma,
            dma,
            dma,
            dma((dates_own,)),
            dma((dates_own,)),
            dma((dates_own,)),
            dma((dates_own,)),
            dma((dates_own,)),
            dma((dates_own,)),
            dma((dates_own,)),
            dma((dates_own,)),
            dma((groups, n_path)),
            dma((n_trade,)),
        ],
        compiler_params=pltpu.CompilerParams(
            collective_id=0, has_side_effects=True, vmem_limit_bytes=61 << 20
        ),
    )(
        factors,
        loadings,
        notional[None],
        strike[None],
        date_weight,
        loss_spanning[None],
        loss_local[None],
        trade_slot[None],
        span_list[None],
    )


def solution(mesh):
    return jax.shard_map(
        functools.partial(on_device, mesh.shape["path"], mesh.shape["trade"]),
        mesh=mesh,
        in_specs=(
            P(None, None, "path"),
            P(None, None, "trade"),
            P("trade"),
            P("trade"),
            P(),
            P(),
            P("trade"),
            P("trade"),
            P("trade"),
        ),
        out_specs=(P("path", None, "trade"), P("trade", None, "path")),
        check_vma=False,
    )
```

profile of v0, /device:TPU:7, one launch (start us, length us, event | category | flops | bytes accessed | tf_op | source)
XLA Modules:
  0.0 62.7 jit_solution(13012519812644449545)
XLA Ops:
  0.6 60.5 %shard_map.104 = (f32[8,8,4096]{2,1,0:T(8,128)S(1)}, f32[4,8,128]{2,1,0:T(8,128)S(1)}) custom-call(bf16[32,8,128]{2,1,0:T(8,128)(2,1)} %factors_ref.1, bf16[32,8,4096]{2,1,0:T(8,128)(2,1)} %loadings_ref.1, f32[1,4096]{1,0:T(1,128)} %bitcast.6, f32[1,4096]{1,0:T(1,128)} %bitcast.7, f32[32]{0:T(128)} %date_weight_ref.1, f32[1,128]{1,0:T(1,128)} %bitcast.9, ...), custom_call_target="tpu_custom_call" | custom-call | tf_op jit(solution)/shard_map/pallas_call | solution.py:375
  61.2 1.0 %copy.13 = f32[8,8,4096]{2,1,0:T(8,128)} copy(f32[8,8,4096]{2,1,0:T(8,128)S(1)} %get-tuple-element.2) | data formatting | bytes 2097152
  62.1 0.6 copy.14
where the time goes:
time: 62.9 us; the launch traced here: 62.7 us
  Pallas kernels  60.5 us (96%)
  local copies, waits for them, and re-layouts  1.58 us (3%)
  between operations  0.64 us (1%)
    pallas_call x1, Pallas kernels, on_device(): pl.pallas_call(functools.partial(kernel, n_path, n_trade), out_shape=(plt...  60.5 us
    unnamed x2, local copies, waits for them, and re-layouts  1.58 us

commit v1 on v0

--- a/solution.py
+++ b/solution.py
@@ -12,6 +12,7 @@
 MESH = pl.DeviceIdType.MESH
 bf16 = jnp.bfloat16
 f32 = jnp.float32
+f8 = jnp.float8_e4m3fn
 
 
 def chunk_of(paths, trades):
@@ -20,31 +21,53 @@
 
 def dot(a, b):
     return jnp.dot(a, b, preferred_element_type=f32)
+
+
+factor_pieces = 4
+loading_pieces = 2
+factor_scale = 2.0**5
+loading_scale = 2.0**9
+
+
+def pieces_of(x, count):
+    pieces = []
+    for _ in range(count):
+        piece = x.astype(f8).astype(f32)
+        pieces.append(piece)
+        x = x - piece
+    return pieces
 
 
 def kernel(
     n_path,
     n_trade,
-    factors_ref,
-    loadings_ref,
-    notional_ref,
-    strike_ref,
-    date_weight_ref,
-    loss_span_ref,
-    loss_local_ref,
-    slot_ref,
-    span_ref,
+    factors_hbm,
+    loadings_hbm,
+    notional_hbm,
+    strike_hbm,
+    date_weight_hbm,
+    loss_span_hbm,
+    loss_local_hbm,
+    slot_hbm,
+    span_hbm,
     loading_grad_ref,
     factor_grad_ref,
     growth,
     table,
     table_t,
     load_own,
-    load_wide,
+    load_split,
+    notional_ref,
+    strike_ref,
     offset,
+    date_weight_ref,
+    loss_span_ref,
+    loss_local_ref,
+    slot_ref,
+    span_ref,
     fac_recv,
     fac,
-    fac_t,
+    fac_split,
     total,
     part,
     pair_recv,
@@ -57,7 +80,8 @@
     factor_acc,
     grad_send,
     grad_recv,
-    load_sem,
+    ready_sem,
+    in_sem,
     fac_ssem,
     fac_rsem,
     pair_ssem,
@@ -73,11 +97,11 @@
 ):
     me_path = lax.axis_index("path")
     me_trade = lax.axis_index("trade")
-    dates, factor_count, path_local = factors_ref.shape
+    dates, factor_count, path_local = factors_hbm.shape
     dates_own = dates // n_path
     dates_out = dates // n_trade
     groups = dates_own // dates_out
-    trades = loadings_ref.shape[2]
+    trades = loadings_hbm.shape[2]
     spans = loss_span_ref.shape[1]
     span_slots = span_ref.shape[1]
     locals_ = loss_local_ref.shape[1]
@@ -104,21 +128,41 @@
     def columns(c):
         return pl.ds(pl.multiple_of(c * chunk, chunk), chunk)
 
-    load = pltpu.make_async_copy(
-        loadings_ref.at[pl.ds(first_date, dates_own)], load_own, load_sem
-    )
-    load.start()
+    def wait_all(buffer, sem):
+        pltpu.make_async_copy(buffer, buffer, sem).wait()
 
     barrier = pltpu.get_barrier_semaphore()
-    for a in range(n_path):
-        for b in range(n_trade):
-            if a or b:
-                pl.semaphore_signal(
-                    barrier,
-                    inc=1,
-                    device_id={"path": path_at(a), "trade": trade_at(b)},
-                    device_id_type=MESH,
-                )
+    for a in range(1, n_path):
+        pl.semaphore_signal(
+            barrier, inc=1, device_id={"path": path_at(a)}, device_id_type=MESH
+        )
+    for b in range(1, n_trade):
+        pl.semaphore_signal(
+            barrier, inc=1, device_id={"trade": trade_at(b)}, device_id_type=MESH
+        )
+
+    own_dates = pl.ds(first_date, dates_own)
+    inputs = [
+        pltpu.make_async_copy(source, target, in_sem.at[i])
+        for i, (source, target) in enumerate(
+            (
+                (slot_hbm, slot_ref),
+                (span_hbm, span_ref),
+                (loadings_hbm.at[own_dates], load_own),
+                (factors_hbm.at[own_dates], fac_recv.at[0]),
+                (notional_hbm, notional_ref),
+                (strike_hbm, strike_ref),
+                (date_weight_hbm, date_weight_ref),
+                (loss_span_hbm, loss_span_ref),
+                (loss_local_hbm, loss_local_ref),
+            )
+        )
+    ]
+    for copy in inputs:
+        copy.start()
+    for copy in inputs[:2]:
+        copy.wait()
+
     set_match = (
         lax.broadcasted_iota(jnp.int32, (spans, span_slots), 0) == span_ref[...]
     ).astype(f32).astype(bf16)
@@ -134,13 +178,16 @@
         table_t[:, cols] = both.astype(bf16)
         table[cols, :] = both.T.astype(bf16)
 
-    pl.semaphore_wait(barrier, n_path * n_trade - 1)
+    for copy in inputs[2:]:
+        copy.wait()
+
+    pl.semaphore_wait(barrier, n_path + n_trade - 2)
 
     def fac_copy(o):
         there = path_at(o)
         return pltpu.make_async_remote_copy(
-            src_ref=factors_ref.at[pl.ds(there * dates_own, dates_own)],
-            dst_ref=fac_recv.at[o - 1],
+            src_ref=factors_hbm.at[pl.ds(there * dates_own, dates_own)],
+            dst_ref=fac_recv.at[o],
             send_sem=fac_ssem,
             recv_sem=fac_rsem,
             device_id={"path": there},
@@ -149,31 +196,65 @@
 
     for o in range(1, n_path):
         fac_copy(o).start()
+    for o in range(1, n_path):
+        pl.semaphore_signal(
+            ready_sem, inc=1, device_id={"path": path_at(o)}, device_id_type=MESH
+        )
 
     offset[...] = notional_ref[...] * strike_ref[...]
-    load.wait()
-
-    for d in range(dates_own):
-        row = load_own[d]
-        load_wide[d] = jnp.concatenate([row, row, row, row], axis=0)
+
+    @pl.loop(0, dates_own)
+    def _(d):
+        pieces = pieces_of(load_own[d].astype(f32) * loading_scale, loading_pieces)
+        load_split[d] = jnp.concatenate(pieces * factor_pieces, axis=0).astype(f8)
+
+    def split_factors(first, last):
+        @pl.loop(0, dates_own)
+        def _(d):
+            for o in range(first, last):
+                block = fac_recv[o, d]
+                at = pl.ds(o * path_local, path_local)
+                fac[d, :, at] = block
+                scaled = block.astype(f32) * f32(math.log2(math.e)) * factor_scale
+                split = [
+                    piece
+                    for piece in pieces_of(scaled, factor_pieces)
+                    for _ in range(loading_pieces)
+                ]
+                fac_split[d, at, :] = jnp.concatenate(split, axis=0).T.astype(f8)
+
+    def phase_one(d, first, last):
+        at = slice(first, last)
+        total[at, :] = jnp.zeros((last - first, total.shape[1]), f32)
+
+        @pl.loop(0, steps, unroll=True)
+        def _(c):
+            cols = columns(c)
+            exponent = dot(fac_split[d, at, :], load_split[d, :, cols])
+            exponent = exponent * (1.0 / (factor_scale * loading_scale))
+            grown = jnp.exp2(exponent) * notional_ref[:, cols]
+            growth[d * steps + c, at, :] = grown.astype(bf16)
+            values = (grown - offset[:, cols]).astype(bf16)
+            total[at, :] += dot(values, table[cols, :])
+
+        for r in range(first // rows, last // rows):
+            part[d, r % 2, r // 2] = total[r * rows : (r + 1) * rows, :spans]
+        weight = date_weight_ref[first_date + d]
+        local_w[d, at, :] = (
+            weight
+            * loss_local_ref[...]
+            * jax.nn.sigmoid(total[at, spans:] / smoothing)
+        ).astype(bf16)
+
+    split_factors(0, 1)
+
+    @pl.loop(0, dates_own)
+    def _(d):
+        phase_one(d, 0, path_local)
 
     if n_path > 1:
-        pltpu.make_async_copy(fac_recv, fac_recv, fac_rsem).wait()
-
-    for d in range(dates_own):
-        blocks = [factors_ref[first_date + d]]
-        blocks += [fac_recv[o - 1, d] for o in range(1, n_path)]
-        whole = jnp.concatenate(blocks, axis=1)
-        fac[d] = whole
-        scaled = whole.astype(f32) * f32(math.log2(math.e))
-        high = scaled.astype(bf16).astype(f32)
-        middle = (scaled - high).astype(bf16).astype(f32)
-        low = scaled - high - middle
-        split = jnp.concatenate([high, middle, low, jnp.zeros_like(low)], axis=0)
-        fac_t[d] = split.T.astype(bf16)
-
-    def wait_all(buffer, sem):
-        pltpu.make_async_copy(buffer, buffer, sem).wait()
+        wait_all(fac_recv.at[pl.ds(1, n_path - 1)], fac_rsem)
+        split_factors(1, n_path)
 
     def send_pair(d):
         pltpu.make_async_remote_copy(
@@ -234,24 +315,9 @@
 
     @pl.loop(0, dates_own)
     def _(d):
-        total[...] = jnp.zeros_like(total)
-
-        @pl.loop(0, steps, unroll=True)
-        def _(c):
-            cols = columns(c)
-            exponent = dot(fac_t[d], load_wide[d, :, cols])
-            grown = jnp.exp2(exponent) * notional_ref[:, cols]
-            growth[d * steps + c] = grown.astype(bf16)
-            values = (grown - offset[:, cols]).astype(bf16)
-            total[...] += dot(values, table[cols, :])
-
-        for r in range(n_trade):
-            part[d, r % 2, r // 2] = total[r * rows : (r + 1) * rows, :spans]
+        if n_path > 1:
+            phase_one(d, path_local, path_total)
         send_pair(d)
-        weight = date_weight_ref[first_date + d]
-        local_w[d] = (
-            weight * loss_local_ref[...] * jax.nn.sigmoid(total[:, spans:] / smoothing)
-        ).astype(bf16)
 
         for late, stage in stages:
 
@@ -269,6 +335,9 @@
             device_id_type=MESH,
         )
 
+    if n_path > 1:
+        pl.semaphore_wait(ready_sem, n_path - 1)
+
     @pl.loop(0, dates_own)
     def _(d):
         wait_all(span_other.at[d], other_rsem.at[d])
@@ -277,17 +346,19 @@
                 start = pl.multiple_of((chip_at(-o) * 2 + core) * rows, rows)
                 slot_w[pl.ds(start, rows), :spans] = source[d, o]
         slot_w[:, spans:] = local_w[d]
-        factor_acc[...] = jnp.zeros_like(factor_acc)
 
         @pl.loop(0, steps, unroll=True)
         def _(c):
-            cols = columns(c)
-            weight = dot(slot_w[...], table_t[:, cols]).astype(bf16)
-            sensitivity = weight * growth[d * steps + c]
-            loading_grad_ref[d, :, cols] = dot(fac[d], sensitivity) / path_total
+            weight = dot(slot_w[...], table_t[:, columns(c)]).astype(bf16)
+            growth[d * steps + c] = weight * growth[d * steps + c]
+
+        factor_acc[...] = jnp.zeros_like(factor_acc)
+
+        @pl.loop(0, steps, unroll=True)
+        def _(c):
             factor_acc[...] += lax.dot_general(
-                load_own[d, :, cols],
-                sensitivity,
+                load_own[d, :, columns(c)],
+                growth[d * steps + c],
                 (((1,), (1,)), ((), ())),
                 preferred_element_type=f32,
             )
@@ -321,8 +392,16 @@
             for o in range(1, n_path):
                 grad_copy(g, o).start()
 
+    @pl.loop(0, dates_own)
+    def _(d):
+        @pl.loop(0, steps, unroll=True)
+        def _(c):
+            loading_grad_ref[d, :, columns(c)] = (
+                dot(fac[d], growth[d * steps + c]) / path_total
+            )
+
     if n_path > 1:
-        wait_all(fac_recv, fac_ssem)
+        wait_all(fac_recv.at[pl.ds(1, n_path - 1)], fac_ssem)
     for d in range(dates_own):
         wait_all(pair_recv.at[d], pair_ssem.at[d])
         wait_all(cross_recv.at[d], cross_ssem.at[d])
@@ -362,6 +441,7 @@
     trades = loadings.shape[2]
     spans = loss_spanning.shape[0]
     locals_ = loss_local.shape[0]
+    span_slots = span_list.shape[0]
     width = spans + locals_
     paths = n_path * path_local
     rows = paths // n_trade
@@ -370,6 +450,7 @@
     dates_out = dates // n_trade
     groups = dates_own // dates_out
     chunk = chunk_of(paths, trades)
+    depth = factor_pieces * loading_pieces * factor_count
     vmem = pl.BlockSpec(memory_space=pltpu.VMEM)
     dma = pltpu.SemaphoreType.DMA
     return pl.pallas_call(
@@ -378,28 +459,25 @@
             pltpu.VMEM((dates_own, factor_count, trades), f32),
             pltpu.VMEM((dates_out, factor_count, path_local), f32),
         ),
-        in_specs=[
-            vmem,
-            pl.BlockSpec(memory_space=pl.ANY),
-            vmem,
-            vmem,
-            pl.BlockSpec(memory_space=pltpu.SMEM),
-            vmem,
-            vmem,
-            vmem,
-            vmem,
-        ],
+        in_specs=[pl.BlockSpec(memory_space=pl.ANY)] * 9,
         out_specs=(vmem, vmem),
         scratch_shapes=[
             pltpu.VMEM((dates_own * (trades // chunk), paths, chunk), bf16),
             pltpu.VMEM((trades, width), bf16),
             pltpu.VMEM((width, trades), bf16),
             pltpu.VMEM((dates_own, factor_count, trades), bf16),
-            pltpu.VMEM((dates_own, 4 * factor_count, trades), bf16),
+            pltpu.VMEM((dates_own, depth, trades), f8),
             pltpu.VMEM((1, trades), f32),
-            pltpu.VMEM((max(n_path - 1, 1), dates_own, factor_count, path_local), bf16),
+            pltpu.VMEM((1, trades), f32),
+            pltpu.VMEM((1, trades), f32),
+            pltpu.SMEM((dates,), f32),
+            pltpu.VMEM((1, spans), f32),
+            pltpu.VMEM((1, locals_), f32),
+            pltpu.VMEM((1, trades), jnp.int32),
+            pltpu.VMEM((1, span_slots), jnp.int32),
+            pltpu.VMEM((n_path, dates_own, factor_count, path_local), bf16),
             pltpu.VMEM((dates_own, factor_count, paths), bf16),
-            pltpu.VMEM((dates_own, paths, 4 * factor_count), bf16),
+            pltpu.VMEM((dates_own, paths, depth), f8),
             pltpu.VMEM((paths, width), f32),
             pltpu.VMEM((dates_own, 2, chips, rows, spans), f32),
             pltpu.VMEM((dates_own, chips, rows, spans), f32),
@@ -412,7 +490,8 @@
             pltpu.VMEM((factor_count, paths), f32),
             pltpu.VMEM((groups, n_path, dates_out, factor_count, path_local), f32),
             pltpu.VMEM((n_trade, dates_out, factor_count, path_local), f32),
-            dma,
+            pltpu.SemaphoreType.REGULAR,
+            dma((9,)),
             dma,
             dma,
             dma((dates_own,)),

time: 62.9 us -> 60.2 us (0.957)
  the two profiles are of different devices: /device:TPU:7 before, /device:TPU:0 now
where the time goes in v1:
time: 60.2 us; the launch traced here: 60 us
  Pallas kernels  57.7 us (96%)
  local copies, waits for them, and re-layouts  1.58 us (3%)
  between operations  0.64 us (1%)
    pallas_call x1, Pallas kernels, on_device(): pl.pallas_call(functools.partial(kernel, n_path, n_trade), out_shape=(plt...  57.7 us
    unnamed x2, local copies, waits for them, and re-layouts  1.58 us

profile of v1, /device:TPU:0, one launch (start us, length us, event | category | flops | bytes accessed | tf_op | source)
XLA Modules:
  0.0 60.0 jit_solution(3878903551663435544)
XLA Ops:
  0.6 57.7 %shard_map.104 = (f32[8,8,4096]{2,1,0:T(8,128)S(1)}, f32[4,8,128]{2,1,0:T(8,128)S(1)}) custom-call(bf16[32,8,128]{2,1,0:T(8,128)(2,1)} %factors_hbm.1, bf16[32,8,4096]{2,1,0:T(8,128)(2,1)} %loadings_hbm.1, f32[1,4096]{1,0:T(1,128)} %bitcast.6, f32[1,4096]{1,0:T(1,128)} %bitcast.7, f32[32]{0:T(128)} %date_weight_hbm.1, f32[1,128]{1,0:T(1,128)} %bitcast.9, ...), custom_call_target="tpu_custom_call" | custom-call | tf_op jit(solution)/shard_map/pallas_call | solution.py:456
  58.4 1.0 %copy.13 = f32[8,8,4096]{2,1,0:T(8,128)} copy(f32[8,8,4096]{2,1,0:T(8,128)S(1)} %get-tuple-element.2) | data formatting | bytes 2097152
  59.3 0.6 %copy.14 = f32[4,8,128]{2,1,0:T(8,128)} copy(f32[4,8,128]{2,1,0:T(8,128)S(1)} %get-tuple-element.3) | data formatting | bytes 32768

commit v2 on v1

--- a/solution.py
+++ b/solution.py
@@ -9,33 +9,18 @@
 from jax.sharding import PartitionSpec as P
 
 smoothing = 0.5
+vmem_bytes = 254 << 18
 MESH = pl.DeviceIdType.MESH
 bf16 = jnp.bfloat16
 f32 = jnp.float32
-f8 = jnp.float8_e4m3fn
 
 
 def chunk_of(paths, trades):
-    return math.gcd(trades, (1 << 20) // paths)
+    return math.gcd(trades, (1 << 21) // paths)
 
 
 def dot(a, b):
     return jnp.dot(a, b, preferred_element_type=f32)
-
-
-factor_pieces = 4
-loading_pieces = 2
-factor_scale = 2.0**5
-loading_scale = 2.0**9
-
-
-def pieces_of(x, count):
-    pieces = []
-    for _ in range(count):
-        piece = x.astype(f8).astype(f32)
-        pieces.append(piece)
-        x = x - piece
-    return pieces
 
 
 def kernel(
@@ -68,7 +53,6 @@
     fac_recv,
     fac,
     fac_split,
-    total,
     part,
     pair_recv,
     chip_sum,
@@ -77,7 +61,6 @@
     span_half,
     span_other,
     slot_w,
-    factor_acc,
     grad_send,
     grad_recv,
     ready_sem,
@@ -205,8 +188,8 @@
 
     @pl.loop(0, dates_own)
     def _(d):
-        pieces = pieces_of(load_own[d].astype(f32) * loading_scale, loading_pieces)
-        load_split[d] = jnp.concatenate(pieces * factor_pieces, axis=0).astype(f8)
+        row = load_own[d]
+        load_split[d] = jnp.concatenate([row, row, row, row], axis=0)
 
     def split_factors(first, last):
         @pl.loop(0, dates_own)
@@ -215,42 +198,42 @@
                 block = fac_recv[o, d]
                 at = pl.ds(o * path_local, path_local)
                 fac[d, :, at] = block
-                scaled = block.astype(f32) * f32(math.log2(math.e)) * factor_scale
-                split = [
-                    piece
-                    for piece in pieces_of(scaled, factor_pieces)
-                    for _ in range(loading_pieces)
-                ]
-                fac_split[d, at, :] = jnp.concatenate(split, axis=0).T.astype(f8)
+                scaled = block.astype(f32) * f32(math.log2(math.e))
+                high = scaled.astype(bf16).astype(f32)
+                middle = (scaled - high).astype(bf16).astype(f32)
+                low = scaled - high - middle
+                split = [high, middle, low, jnp.zeros_like(low)]
+                fac_split[d, at, :] = jnp.concatenate(split, axis=0).T.astype(bf16)
 
     def phase_one(d, first, last):
         at = slice(first, last)
-        total[at, :] = jnp.zeros((last - first, total.shape[1]), f32)
-
-        @pl.loop(0, steps, unroll=True)
-        def _(c):
-            cols = columns(c)
+        total = None
+        for c in range(steps):
+            cols = slice(c * chunk, (c + 1) * chunk)
             exponent = dot(fac_split[d, at, :], load_split[d, :, cols])
-            exponent = exponent * (1.0 / (factor_scale * loading_scale))
             grown = jnp.exp2(exponent) * notional_ref[:, cols]
             growth[d * steps + c, at, :] = grown.astype(bf16)
             values = (grown - offset[:, cols]).astype(bf16)
-            total[at, :] += dot(values, table[cols, :])
+            sums = dot(values, table[cols, :])
+            total = sums if total is None else total + sums
 
         for r in range(first // rows, last // rows):
-            part[d, r % 2, r // 2] = total[r * rows : (r + 1) * rows, :spans]
+            here = slice(r * rows - first, (r + 1) * rows - first)
+            part[d, r % 2, r // 2] = total[here, :spans]
         weight = date_weight_ref[first_date + d]
         local_w[d, at, :] = (
             weight
             * loss_local_ref[...]
-            * jax.nn.sigmoid(total[at, spans:] / smoothing)
+            * jax.nn.sigmoid(total[:, spans:] / smoothing)
         ).astype(bf16)
 
     split_factors(0, 1)
-
-    @pl.loop(0, dates_own)
-    def _(d):
-        phase_one(d, 0, path_local)
+    unroll = math.gcd(dates_own, 4)
+
+    @pl.loop(0, dates_own // unroll)
+    def _(block):
+        for i in range(unroll):
+            phase_one(block * unroll + i, 0, path_local)
 
     if n_path > 1:
         wait_all(fac_recv.at[pl.ds(1, n_path - 1)], fac_rsem)
@@ -311,19 +294,22 @@
         ).start()
 
     lag = max(1, (dates_own - 1) // 3)
-    stages = ((lag, send_cross), (2 * lag, send_half), (3 * lag, send_other))
+    stages = ((max(1, lag // 2), send_cross), (2 * lag, send_half), (3 * lag, send_other))
+
+    def exchange(turn):
+        for late, done in stages:
+            d = turn - late
+
+            @pl.when(jnp.logical_and(d >= 0, d < dates_own))
+            def _(d=d, done=done):
+                done(d)
 
     @pl.loop(0, dates_own)
     def _(d):
         if n_path > 1:
             phase_one(d, path_local, path_total)
         send_pair(d)
-
-        for late, stage in stages:
-
-            @pl.when(d >= late)
-            def _(late=late, stage=stage):
-                stage(d - late)
+        exchange(d)
 
     def grad_copy(g, o):
         return pltpu.make_async_remote_copy(
@@ -338,8 +324,7 @@
     if n_path > 1:
         pl.semaphore_wait(ready_sem, n_path - 1)
 
-    @pl.loop(0, dates_own)
-    def _(d):
+    def gather_weights(d):
         wait_all(span_other.at[d], other_rsem.at[d])
         for o in range(chips):
             for core, source in ((me_core, span_half), (1 - me_core, span_other)):
@@ -347,33 +332,29 @@
                 slot_w[pl.ds(start, rows), :spans] = source[d, o]
         slot_w[:, spans:] = local_w[d]
 
-        @pl.loop(0, steps, unroll=True)
-        def _(c):
-            weight = dot(slot_w[...], table_t[:, columns(c)]).astype(bf16)
+    def sensitivities(d):
+        for c in range(steps):
+            cols = slice(c * chunk, (c + 1) * chunk)
+            weight = dot(slot_w[...], table_t[:, cols]).astype(bf16)
             growth[d * steps + c] = weight * growth[d * steps + c]
 
-        factor_acc[...] = jnp.zeros_like(factor_acc)
-
-        @pl.loop(0, steps, unroll=True)
-        def _(c):
-            factor_acc[...] += lax.dot_general(
-                load_own[d, :, columns(c)],
+    def factor_gradient(d):
+        total = None
+        for c in range(steps):
+            sums = lax.dot_general(
+                load_own[d, :, c * chunk : (c + 1) * chunk],
                 growth[d * steps + c],
                 (((1,), (1,)), ((), ())),
                 preferred_element_type=f32,
             )
-
-        g = d // dates_out
+            total = sums if total is None else total + sums
         for o in range(n_path):
-            grad_send[g, o, lax.rem(d, dates_out)] = factor_acc[
+            grad_send[d // dates_out, o, lax.rem(d, dates_out)] = total[
                 :, o * path_local : (o + 1) * path_local
             ]
 
-        for late, stage in stages:
-
-            @pl.when(d < late)
-            def _(late=late, stage=stage):
-                stage(d + dates_own - late)
+    def send_gradient(d):
+        g = d // dates_out
 
         @pl.when(lax.rem(d, dates_out) == dates_out - 1)
         def _():
@@ -392,13 +373,29 @@
             for o in range(1, n_path):
                 grad_copy(g, o).start()
 
-    @pl.loop(0, dates_own)
+    gather_weights(0)
+    sensitivities(0)
+    exchange(jnp.int32(dates_own))
+
+    @pl.loop(1, dates_own)
     def _(d):
-        @pl.loop(0, steps, unroll=True)
-        def _(c):
-            loading_grad_ref[d, :, columns(c)] = (
-                dot(fac[d], growth[d * steps + c]) / path_total
-            )
+        gather_weights(d)
+        factor_gradient(d - 1)
+        sensitivities(d)
+        exchange(dates_own + d)
+        send_gradient(d - 1)
+
+    factor_gradient(jnp.int32(dates_own - 1))
+    send_gradient(jnp.int32(dates_own - 1))
+
+    @pl.loop(0, dates_own // unroll)
+    def _(block):
+        for i in range(unroll):
+            d = block * unroll + i
+            for c in range(steps):
+                loading_grad_ref[d, :, c * chunk : (c + 1) * chunk] = (
+                    dot(fac[d], growth[d * steps + c]) / path_total
+                )
 
     if n_path > 1:
         wait_all(fac_recv.at[pl.ds(1, n_path - 1)], fac_ssem)
@@ -450,7 +447,8 @@
     dates_out = dates // n_trade
     groups = dates_own // dates_out
     chunk = chunk_of(paths, trades)
-    depth = factor_pieces * loading_pieces * factor_count
+    depth = 4 * factor_count
+    results = 4 * factor_count * (dates_own * trades + dates_out * path_local)
     vmem = pl.BlockSpec(memory_space=pltpu.VMEM)
     dma = pltpu.SemaphoreType.DMA
     return pl.pallas_call(
@@ -466,7 +464,7 @@
             pltpu.VMEM((trades, width), bf16),
             pltpu.VMEM((width, trades), bf16),
             pltpu.VMEM((dates_own, factor_count, trades), bf16),
-            pltpu.VMEM((dates_own, depth, trades), f8),
+            pltpu.VMEM((dates_own, depth, trades), bf16),
             pltpu.VMEM((1, trades), f32),
             pltpu.VMEM((1, trades), f32),
             pltpu.VMEM((1, trades), f32),
@@ -477,8 +475,7 @@
             pltpu.VMEM((1, span_slots), jnp.int32),
             pltpu.VMEM((n_path, dates_own, factor_count, path_local), bf16),
             pltpu.VMEM((dates_own, factor_count, paths), bf16),
-            pltpu.VMEM((dates_own, paths, depth), f8),
-            pltpu.VMEM((paths, width), f32),
+            pltpu.VMEM((dates_own, paths, depth), bf16),
             pltpu.VMEM((dates_own, 2, chips, rows, spans), f32),
             pltpu.VMEM((dates_own, chips, rows, spans), f32),
             pltpu.VMEM((dates_own, chips, rows, spans), f32),
@@ -487,7 +484,6 @@
             pltpu.VMEM((dates_own, chips, rows, spans), bf16),
             pltpu.VMEM((dates_own, chips, rows, spans), bf16),
             pltpu.VMEM((paths, width), bf16),
-            pltpu.VMEM((factor_count, paths), f32),
             pltpu.VMEM((groups, n_path, dates_out, factor_count, path_local), f32),
             pltpu.VMEM((n_trade, dates_out, factor_count, path_local), f32),
             pltpu.SemaphoreType.REGULAR,
@@ -506,7 +502,7 @@
             dma((n_trade,)),
         ],
         compiler_params=pltpu.CompilerParams(
-            collective_id=0, has_side_effects=True, vmem_limit_bytes=61 << 20
+            collective_id=0, has_side_effects=True, vmem_limit_bytes=vmem_bytes - results
         ),
     )(
         factors,

time: 60.2 us -> 56.9 us (0.945)
  Pallas kernels: 57.7 us -> 54.4 us
    pallas_call x1, Pallas kernels: 57.7 us -> 54.4 us  [on_device(): pl.pallas_call(functools.partial(kernel, n_path, n_trade), out_shape=(plt...]
where the time goes in v2:
time: 56.9 us; the launch traced here: 56.7 us
  Pallas kernels  54.4 us (96%)
  local copies, waits for them, and re-layouts  1.58 us (3%)
  between operations  0.64 us (1%)
    pallas_call x1, Pallas kernels, on_device(): pl.pallas_call(functools.partial(kernel, n_path, n_trade), out_shape=(plt...  54.4 us
    unnamed x2, local copies, waits for them, and re-layouts  1.58 us

profile of v2, /device:TPU:0, one launch (start us, length us, event | category | flops | bytes accessed | tf_op | source)
XLA Modules:
  0.0 56.7 jit_solution(4066855655011544814)
XLA Ops:
  0.6 54.4 %shard_map.104 = (f32[8,8,4096]{2,1,0:T(8,128)S(1)}, f32[4,8,128]{2,1,0:T(8,128)S(1)}) custom-call(bf16[32,8,128]{2,1,0:T(8,128)(2,1)} %factors_hbm.1, bf16[32,8,4096]{2,1,0:T(8,128)(2,1)} %loadings_hbm.1, f32[1,4096]{1,0:T(1,128)} %bitcast.6, f32[1,4096]{1,0:T(1,128)} %bitcast.7, f32[32]{0:T(128)} %date_weight_hbm.1, f32[1,128]{1,0:T(1,128)} %bitcast.9, ...), custom_call_target="tpu_custom_call" | custom-call | tf_op jit(solution)/shard_map/pallas_call | solution.py:454
  55.1 1.0 %copy.13 = f32[8,8,4096]{2,1,0:T(8,128)} copy(f32[8,8,4096]{2,1,0:T(8,128)S(1)} %get-tuple-element.2) | data formatting | bytes 2097152
  56.1 0.6 %copy.14 = f32[4,8,128]{2,1,0:T(8,128)} copy(f32[4,8,128]{2,1,0:T(8,128)S(1)} %get-tuple-element.3) | data formatting | bytes 32768

commit v3 on v2

--- a/solution.py
+++ b/solution.py
@@ -17,6 +17,27 @@
 
 def chunk_of(paths, trades):
     return math.gcd(trades, (1 << 21) // paths)
+
+
+def gathered_of(chunk):
+    return (chunk // 4) // 128 * 128
+
+
+def lane_gather(x, index):
+    numbers = lax.GatherDimensionNumbers(
+        offset_dims=(),
+        collapsed_slice_dims=(1,),
+        start_index_map=(1,),
+        operand_batching_dims=(0,),
+        start_indices_batching_dims=(0,),
+    )
+    return lax.gather(
+        x,
+        index[..., None],
+        numbers,
+        (1, 1),
+        mode=lax.GatherScatterMode.PROMISE_IN_BOUNDS,
+    )
 
 
 def dot(a, b):
@@ -40,6 +61,7 @@
     growth,
     table,
     table_t,
+    place,
     load_own,
     load_split,
     notional_ref,
@@ -161,6 +183,18 @@
         table_t[:, cols] = both.astype(bf16)
         table[cols, :] = both.T.astype(bf16)
 
+    for c in range(steps):
+        for k in range((c + 1) * chunk - gathered_of(chunk), (c + 1) * chunk, 128):
+            slot = jnp.broadcast_to(slot_ref[:, k : k + 128], (8, 128))
+            column = slot - span_slots + spans
+            for at in range(0, span_slots, 128):
+                row = jnp.broadcast_to(span_ref[:, at : at + 128], (8, 128))
+                span = lane_gather(row, jnp.bitwise_and(slot, 127))
+                here = jnp.logical_and(slot >= at, slot < at + 128)
+                column = jnp.where(here, span, column)
+            place[0:1, k : k + 128] = jnp.bitwise_and(column, 127)[0:1]
+            place[1:2, k : k + 128] = jnp.right_shift(column, 7)[0:1]
+
     for copy in inputs[2:]:
         copy.wait()
 
@@ -333,10 +367,25 @@
         slot_w[:, spans:] = local_w[d]
 
     def sensitivities(d):
+        i16 = jnp.int16
+        block = min(128, path_total)
+        dense = chunk - gathered_of(chunk)
         for c in range(steps):
-            cols = slice(c * chunk, (c + 1) * chunk)
+            now = growth.at[d * steps + c]
+            for k in range(dense, chunk, 128):
+                cols = slice(c * chunk + k, c * chunk + k + 128)
+                lane = jnp.broadcast_to(place[0:1, cols], (block, 128)).astype(i16)
+                group = jnp.broadcast_to(place[1:2, cols], (block, 128)).astype(i16)
+                for r in range(0, path_total, block):
+                    at = slice(r, r + block)
+                    weight = lane_gather(slot_w[at, :128], lane)
+                    for g in range(1, (spans + locals_) // 128):
+                        other = lane_gather(slot_w[at, g * 128 : (g + 1) * 128], lane)
+                        weight = jnp.where(group == g, other, weight)
+                    now[at, k : k + 128] = weight * now[at, k : k + 128]
+            cols = slice(c * chunk, c * chunk + dense)
             weight = dot(slot_w[...], table_t[:, cols]).astype(bf16)
-            growth[d * steps + c] = weight * growth[d * steps + c]
+            now[:, :dense] = weight * now[:, :dense]
 
     def factor_gradient(d):
         total = None
@@ -463,6 +512,7 @@
             pltpu.VMEM((dates_own * (trades // chunk), paths, chunk), bf16),
             pltpu.VMEM((trades, width), bf16),
             pltpu.VMEM((width, trades), bf16),
+            pltpu.VMEM((2, trades), jnp.int32),
             pltpu.VMEM((dates_own, factor_count, trades), bf16),
             pltpu.VMEM((dates_own, depth, trades), bf16),
             pltpu.VMEM((1, trades), f32),

time: 56.9 us -> 55.9 us (0.982)
  Pallas kernels: 54.4 us -> 53.5 us
    pallas_call x1, Pallas kernels: 54.4 us -> 53.5 us  [on_device(): pl.pallas_call(functools.partial(kernel, n_path, n_trade), out_shape=(plt...]
where the time goes in v3:
time: 55.9 us; the launch traced here: 55.7 us
  Pallas kernels  53.5 us (96%)
  local copies, waits for them, and re-layouts  1.58 us (3%)
  between operations  0.64 us (1%)
    pallas_call x1, Pallas kernels, on_device(): pl.pallas_call(functools.partial(kernel, n_path, n_trade), out_shape=(plt...  53.5 us
    unnamed x2, local copies, waits for them, and re-layouts  1.58 us

profile of v3, /device:TPU:0, one launch (start us, length us, event | category | flops | bytes accessed | tf_op | source)
XLA Modules:
  0.0 55.7 jit_solution(13351247745431568184)
XLA Ops:
  0.6 53.5 %shard_map.104 = (f32[8,8,4096]{2,1,0:T(8,128)S(1)}, f32[4,8,128]{2,1,0:T(8,128)S(1)}) custom-call(bf16[32,8,128]{2,1,0:T(8,128)(2,1)} %factors_hbm.1, bf16[32,8,4096]{2,1,0:T(8,128)(2,1)} %loadings_hbm.1, f32[1,4096]{1,0:T(1,128)} %bitcast.6, f32[1,4096]{1,0:T(1,128)} %bitcast.7, f32[32]{0:T(128)} %date_weight_hbm.1, f32[1,128]{1,0:T(1,128)} %bitcast.9, ...), custom_call_target="tpu_custom_call" | custom-call | tf_op jit(solution)/shard_map/pallas_call | solution.py:503
  54.1 1.0 %copy.13 = f32[8,8,4096]{2,1,0:T(8,128)} copy(f32[8,8,4096]{2,1,0:T(8,128)S(1)} %get-tuple-element.2) | data formatting | bytes 2097152
  55.1 0.6 %copy.14 = f32[4,8,128]{2,1,0:T(8,128)} copy(f32[4,8,128]{2,1,0:T(8,128)S(1)} %get-tuple-element.3) | data formatting | bytes 32768

commit v4 on v3

--- a/solution.py
+++ b/solution.py
@@ -20,7 +20,7 @@
 
 
 def gathered_of(chunk):
-    return (chunk // 4) // 128 * 128
+    return (3 * chunk // 8) // 128 * 128
 
 
 def lane_gather(x, index):

time: 55.9 us -> 55.4 us (level)
  no operation moved by 1% of the time
where the time goes in v4:
time: 55.4 us; the launch traced here: 55.2 us
  Pallas kernels  53 us (96%)
  local copies, waits for them, and re-layouts  1.58 us (3%)
  between operations  0.64 us (1%)
    pallas_call x1, Pallas kernels, on_device(): pl.pallas_call(functools.partial(kernel, n_path, n_trade), out_shape=(plt...  53 us
    unnamed x2, local copies, waits for them, and re-layouts  1.58 us

profile of v4, /device:TPU:0, one launch (start us, length us, event | category | flops | bytes accessed | tf_op | source)
XLA Modules:
  0.0 55.2 jit_solution(11011620425572367007)
XLA Ops:
  0.6 53.0 %shard_map.104 = (f32[8,8,4096]{2,1,0:T(8,128)S(1)}, f32[4,8,128]{2,1,0:T(8,128)S(1)}) custom-call(bf16[32,8,128]{2,1,0:T(8,128)(2,1)} %factors_hbm.1, bf16[32,8,4096]{2,1,0:T(8,128)(2,1)} %loadings_hbm.1, f32[1,4096]{1,0:T(1,128)} %bitcast.6, f32[1,4096]{1,0:T(1,128)} %bitcast.7, f32[32]{0:T(128)} %date_weight_hbm.1, f32[1,128]{1,0:T(1,128)} %bitcast.9, ...), custom_call_target="tpu_custom_call" | custom-call | tf_op jit(solution)/shard_map/pallas_call | solution.py:503
  53.6 1.0 %copy.13 = f32[8,8,4096]{2,1,0:T(8,128)} copy(f32[8,8,4096]{2,1,0:T(8,128)S(1)} %get-tuple-element.2) | data formatting | bytes 2097152
  54.6 0.6 %copy.14 = f32[4,8,128]{2,1,0:T(8,128)} copy(f32[4,8,128]{2,1,0:T(8,128)S(1)} %get-tuple-element.3) | data formatting | bytes 32768
